TPU v7x, 32 devices: a whole 2x2x4 slice. The times are simulated.
32 devices in a mesh: dp: 8 (over y, x, core), tensor: 4 (over z).
Axes of the slice: x: 2, y: 2, z: 4, core: 2. Of those that a mesh axis runs over, the one named last changes fastest.
Arguments:
- inputs: bfloat16 [16384, 768], P('dp'), may hold values from -6 to 6
- w_qkv: bfloat16 [768, 3, 768], P(None, None, 'tensor'), may hold values from -0.3125 to 0.3125
- b_qv: float32 [2, 768], P(None, 'tensor'), may hold values from -3 to 3
- w_out: bfloat16 [768, 768], P('tensor'), may hold values from -1.25 to 1.25
- b_out: float32 [768], replicated, may hold values from -3 to 3
- g_one: float32 [768], replicated, may hold values from 0.5 to 1.5
- s_one: float32 [768], replicated, may hold values from -3 to 3
- w_up: bfloat16 [768, 3072], P(None, 'tensor'), may hold values from -0.21875 to 0.21875
- b_up: float32 [3072], P('tensor'), may hold values from -3 to 3
- w_down: bfloat16 [3072, 768], P('tensor'), may hold values from -0.15625 to 0.15625
- b_down: float32 [768], replicated, may hold values from -3 to 3
- g_two: float32 [768], replicated, may hold values from 0.5 to 1.5
- s_two: float32 [768], replicated, may hold values from -3 to 3
- cotangent: bfloat16 [16384, 768], P('dp'), may hold values from -6 to 6
- pad_mask: int32 [16384], P('dp'), may hold values 0 or 1
- doc_lengths: int32 [32], P('dp'), may hold values from 30 to 512, as said below
Outputs:
- out: bfloat16 [16384, 768], P('dp')
- d_inputs: float32 [16384, 768], P('dp')
- d_w_qkv: float32 [768, 3, 768], P(None, None, 'tensor')
- d_b_qv: float32 [2, 768], P(None, 'tensor')
- d_w_out: float32 [768, 768], P('tensor')
- d_b_out: float32 [768], replicated
- d_g_one: float32 [768], replicated
- d_s_one: float32 [768], replicated
- d_w_up: float32 [768, 3072], P(None, 'tensor')
- d_b_up: float32 [3072], P('tensor')
- d_w_down: float32 [3072, 768], P('tensor')
- d_b_down: float32 [768], replicated
- d_g_two: float32 [768], replicated
- d_s_two: float32 [768], replicated
Inputs may be any that keep to these rules, and one draw needn't show every extreme that they name: `doc_lengths`: in every draw one document has 512 true tokens and one has 30. Rows at or beyond a document's count are padding: they are no keys whatever pad_mask says, and their outputs are zero. The first token of a document is always a key.
All inputs are finite; a program needn't handle non-finite values. No bound on the sum of `pad_mask` on one device may be relied on, other than what follows from the above.
Results may differ from a plain program's by a relative error of at most 0.014.
The roundings to bfloat16 on the way count: a program that leaves them out, or rounds other values in their place, can miss the bound.
Values may be sent and summed in bfloat16 or wider, within the bound.
No kernel may reach another device: no remote copies, remote signals or barrier semaphores. Data moves between devices by JAX's collectives and lax.ppermute only.
A program may use at most 128 MiB of HBM per device.

v0:
```python
import jax
import jax.numpy as jnp
from jax import lax
from jax.sharding import PartitionSpec as P

HD = 64


def norm_layer(values, gain, shift):
    center = values - jnp.mean(values, axis=-1, keepdims=True)
    spread = jnp.mean(center * center, axis=-1, keepdims=True)
    return center * lax.rsqrt(spread + 1e-05) * gain + shift


def gelu_exact(values):
    return jax.nn.gelu(values, approximate=False)


def masked_scores(queries, key_rows, key_valid):
    scores = jnp.einsum("qhe,khe->hqk", queries, key_rows, preferred_element_type=jnp.float32)
    return jnp.where(key_valid[None, None, :], scores, -1e30)


def doc_forward(packed):
    queries, key_rows, values, key_valid = packed
    scores = masked_scores(queries, key_rows, key_valid)
    log_total = jax.nn.logsumexp(scores, axis=-1, keepdims=True)
    weights = jnp.exp(scores - log_total).astype(jnp.bfloat16)
    context = jnp.einsum("hqk,khe->qhe", weights, values, preferred_element_type=jnp.float32)
    return (context.astype(jnp.bfloat16), log_total)


def doc_backward(packed):
    queries, key_rows, values, key_valid, log_total, d_context = packed
    scores = masked_scores(queries, key_rows, key_valid)
    weights = jnp.exp(scores - log_total)
    d_prob = jnp.einsum("qhe,khe->hqk", d_context, values, preferred_element_type=jnp.float32)
    d_values = jnp.einsum(
        "hqk,qhe->khe", weights.astype(jnp.bfloat16), d_context, preferred_element_type=jnp.float32
    )
    d_scores = (weights * (d_prob - jnp.sum(d_prob * weights, axis=-1, keepdims=True))).astype(
        jnp.bfloat16
    )
    d_query = jnp.einsum("hqk,khe->qhe", d_scores, key_rows, preferred_element_type=jnp.float32)
    d_keys = jnp.einsum("hqk,qhe->khe", d_scores, queries, preferred_element_type=jnp.float32)
    return (
        d_query.astype(jnp.bfloat16),
        d_keys.astype(jnp.bfloat16),
        d_values.astype(jnp.bfloat16),
    )


def per_device(
    inputs,
    w_qkv,
    b_qv,
    w_out,
    b_out,
    g_one,
    s_one,
    w_up,
    b_up,
    w_down,
    b_down,
    g_two,
    s_two,
    cotangent,
    pad_mask,
    doc_lengths,
):
    rows = inputs.shape[0]
    doc_count = doc_lengths.shape[0]
    length = rows // doc_count
    local_heads = w_qkv.shape[2] // HD
    scale = HD ** (-0.5)
    position = jnp.arange(length, dtype=jnp.int32)
    inside = position[None, :] < doc_lengths[:, None]
    key_valid = inside & ((pad_mask.reshape(doc_count, length) == 1) | (position[None, :] == 0))
    row_weight = inside.astype(jnp.float32).reshape(rows, 1)
    projected = jnp.einsum("td,dce->tce", inputs, w_qkv, preferred_element_type=jnp.float32)
    queries = ((projected[:, 0] + b_qv[0]) * scale).astype(jnp.bfloat16)
    key_rows = projected[:, 1].astype(jnp.bfloat16)
    values = (projected[:, 2] + b_qv[1]).astype(jnp.bfloat16)
    shaped = (doc_count, length, local_heads, HD)
    queries_doc = queries.reshape(shaped)
    keys_doc = key_rows.reshape(shaped)
    values_doc = values.reshape(shaped)
    context, log_total = lax.map(doc_forward, (queries_doc, keys_doc, values_doc, key_valid))
    context = context.reshape(rows, local_heads * HD)
    heads_part = jnp.dot(context, w_out, preferred_element_type=jnp.float32)
    attn = lax.psum(heads_part, "tensor")
    z_one = inputs.astype(jnp.float32) + attn + b_out
    h_one, pull_one = jax.vjp(norm_layer, z_one, g_one, s_one)
    h_low = h_one.astype(jnp.bfloat16)
    up_value = jnp.dot(h_low, w_up, preferred_element_type=jnp.float32) + b_up
    act, pull_act = jax.vjp(gelu_exact, up_value)
    act_low = act.astype(jnp.bfloat16)
    down_part = jnp.dot(act_low, w_down, preferred_element_type=jnp.float32)
    down = lax.psum(down_part, "tensor")
    z_two = h_one + down + b_down
    normed, pull_two = jax.vjp(norm_layer, z_two, g_two, s_two)
    d_ztwo, d_gtwo, d_stwo = pull_two(cotangent.astype(jnp.float32) * row_weight)
    d_bdown = jnp.sum(d_ztwo, axis=0)
    result = (normed * row_weight).astype(jnp.bfloat16)
    dz_two_low = d_ztwo.astype(jnp.bfloat16)
    d_wdown = jnp.einsum("tf,td->fd", act_low, dz_two_low, preferred_element_type=jnp.float32)
    d_act = jnp.einsum("td,fd->tf", dz_two_low, w_down, preferred_element_type=jnp.float32)
    d_up_low = pull_act(d_act)[0].astype(jnp.bfloat16)
    d_bup = jnp.sum(d_up_low, axis=0, dtype=jnp.float32)
    d_wup = jnp.einsum("td,tf->df", h_low, d_up_low, preferred_element_type=jnp.float32)
    hone_part = jnp.einsum("tf,df->td", d_up_low, w_up, preferred_element_type=jnp.float32)
    d_hone = lax.psum(hone_part, "tensor") + d_ztwo
    d_zone, d_gone, d_sone = pull_one(d_hone)
    d_bout = jnp.sum(d_zone, axis=0)
    dz_one_low = d_zone.astype(jnp.bfloat16)
    d_wout = jnp.einsum("th,td->hd", context, dz_one_low, preferred_element_type=jnp.float32)
    d_context = jnp.einsum(
        "td,hd->th", dz_one_low, w_out, preferred_element_type=jnp.float32
    ).astype(jnp.bfloat16)
    back_items = (
        queries_doc,
        keys_doc,
        values_doc,
        key_valid,
        log_total,
        d_context.reshape(shaped),
    )
    d_query, d_keys, d_values = lax.map(doc_backward, back_items)
    d_query = d_query.reshape(rows, local_heads * HD) * jnp.asarray(scale, jnp.bfloat16)
    stacked = jnp.stack(
        [d_query, d_keys.reshape(rows, local_heads * HD), d_values.reshape(rows, local_heads * HD)],
        axis=1,
    )
    d_wqkv = jnp.einsum("td,tce->dce", inputs, stacked, preferred_element_type=jnp.float32)
    d_bqv = jnp.stack(
        [
            jnp.sum(stacked[:, 0], axis=0, dtype=jnp.float32),
            jnp.sum(stacked[:, 2], axis=0, dtype=jnp.float32),
        ]
    )
    input_part = jnp.einsum("tce,dce->td", stacked, w_qkv, preferred_element_type=jnp.float32)
    d_inputs = lax.psum(input_part, "tensor") + d_zone
    summed = lax.psum(
        (
            d_wqkv,
            d_bqv,
            d_wout,
            d_bout,
            d_gone,
            d_sone,
            d_wup,
            d_bup,
            d_wdown,
            d_bdown,
            d_gtwo,
            d_stwo,
        ),
        "dp",
    )
    return (
        result,
        d_inputs,
        summed[0],
        summed[1],
        summed[2],
        summed[3],
        summed[4],
        summed[5],
        summed[6],
        summed[7],
        summed[8],
        summed[9],
        summed[10],
        summed[11],
    )


def solution(mesh):
    placed = (
        P("dp", None),
        P(None, None, "tensor"),
        P(None, "tensor"),
        P("tensor", None),
        P(),
        P(),
        P(),
        P(None, "tensor"),
        P("tensor"),
        P("tensor", None),
        P(),
        P(),
        P(),
        P("dp", None),
        P("dp"),
        P("dp"),
    )
    return jax.shard_map(
        per_device,
        mesh=mesh,
        in_specs=placed,
        out_specs=(
            P("dp", None),
            P("dp", None),
            P(None, None, "tensor"),
            P(None, "tensor"),
            P("tensor", None),
            P(),
            P(),
            P(),
            P(None, "tensor"),
            P("tensor"),
            P("tensor", None),
            P(),
            P(),
            P(),
        ),
        check_vma=False,
    )
```

profile of v0, /device:TPU:0, one launch (start us, length us, event | category | flops | bytes accessed | tf_op | source)
XLA Modules:
  0.0 1201.6 jit_solution(13847251560515117021)
XLA Ops:
  7.2 4.2 fusion.90
  13.5 3.1 squeeze.34
  16.6 2.2 squeeze.35
  21.1 2.9 fusion.73
  25.0 13.6 %while.26 = (s32[]{:T(128)}, bf16[4,512,3,64]{1,3,2,0:T(8,128)(2,1)}, f32[4,3,512,1]{2,1,3,0:T(4,128)}, bf16[4,512,3,64]{1,3,2,0:T(8,128)(2,1)S(1)}, pred[4,512]...) while((s32[]{:T(128)}, ...), condition=%wide.region_3.4_spmd, body=%wide.region_0.3_spmd.sunk | while | flops 207728640 | bytes 10306649 | solution.py:88
  30.3 1.5 fusion.134
  38.6 2.0 copy.49
  41.7 4.7 fusion.91
  46.9 225.2 %all-reduce.8.cloned.1.call-done = f32[2048,768]{1,0:T(8,128)} async-done(((f32[2048,768]{1,0:T(8,128)}), f32[2048,768]{1,0:T(8,128)}) %all-reduce.8.cloned.1.call-update) | async-done | bytes 6291472 | tf_op jit(solution)/shard_map/psum | solution.py:91
  272.2 4.6 fusion.88
  279.4 18.3 %multiply_convert_fusion.2 = (bf16[2048,768]{1,0:T(8,128)(2,1)S(1)}, f32[2048,768]{1,0:T(8,128)}, f32[2048,768]{1,0:T(8,128)}) fusion(f32[768]{0:T(1024)S(1)} %copy-done.35, bf16[2048,768]{1,0:T(8,128)(2,1)S(1)} %fusion.69, bf16[768,768]{1,0:T(8,128)(2,1)S(1)} %copy-done), kind=kOutput, calls=%fused_computation.84 | convolution fusion | flops 2519728128 | bytes 20057088 | tf_op jit(solution)/shard_map/dot_general | solution.py:95
  297.8 1.8 copy-done.37
  299.5 4.5 fusion.92
  304.2 221.7 %all-reduce.10.cloned.1.call-done = f32[2048,768]{1,0:T(8,128)} async-done(((f32[2048,768]{1,0:T(8,128)}), f32[2048,768]{1,0:T(8,128)}) %all-reduce.10.cloned.1.call-update) | async-done | bytes 6291472 | tf_op jit(solution)/shard_map/psum | solution.py:99
  525.9 5.7 fusion.86
  533.5 3.6 multiply_reduce_fusion.1
  537.2 4.9 fusion.85
  542.1 9.3 convert_reduce_fusion
  551.4 1.7 copy-done.36
  553.1 4.5 fusion.93
  557.9 221.6 %all-reduce.12.cloned.1.call-done = f32[2048,768]{1,0:T(8,128)} async-done(((f32[2048,768]{1,0:T(8,128)}), f32[2048,768]{1,0:T(8,128)}) %all-reduce.12.cloned.1.call-update) | async-done | bytes 6291472 | tf_op jit(solution)/shard_map/psum | solution.py:112
  779.5 8.7 multiply_reduce_fusion.2
  788.3 4.3 fusion.84
  792.6 2.7 copy-done.3
  799.3 30.5 %while.27 = (s32[]{:T(128)}, bf16[4,512,3,64]{1,3,2,0:T(8,128)(2,1)S(1)}, bf16[4,512,3,64]{1,3,2,0:T(8,128)(2,1)}, bf16[4,512,3,64]{1,3,2,0:T(8,128)(2,1)S(1)}, ...) while((s32[]{:T(128)}, ...), condition=%wide.region_17.18_spmd, body=%wide.region_15.17_spmd.sunk | while | flops 513047040 | bytes 25611892 | solution.py:128
  800.7 2.0 multiply_reduce_fusion.8
  805.2 1.7 fusion.147
  808.3 2.0 multiply_reduce_fusion.8
  812.8 1.7 fusion.147
  816.0 2.0 multiply_reduce_fusion.8
  820.5 1.7 fusion.147
  823.6 2.0 multiply_reduce_fusion.8
  828.1 1.7 fusion.147
  830.6 1.5 mul.219
  832.0 2.1 constant_dynamic-update-slice_fusion.2
  835.3 1.5 copy.54
  836.8 2.3 stack_reshape.7
  841.1 7.2 convolution_bitcast_fusion
  848.3 7.1 fusion.94
  855.4 7.1 fusion.81
  862.6 1.8 fusion.83
  865.4 3.2 fusion.75
  870.1 200.1 %all-reduce.14.cloned.1.call-done = f32[2048,768]{1,0:T(8,128)} async-done(((f32[2048,768]{1,0:T(8,128)}), f32[2048,768]{1,0:T(8,128)}) %all-reduce.14.cloned.1.call-update) | async-done | bytes 6291472 | tf_op jit(solution)/shard_map/psum | solution.py:142
  1070.1 7.7 add_reduce_fusion
  1077.8 26.2 %all-reduce = (f32[2,192]{1,0:T(2,128)}, f32[768]{0:T(1024)}, f32[768]{0:T(1024)}, f32[768]{0:T(1024)}, f32[768]{0:T(1024)}, /*index=5*/f32[768]{0:T(1024)}, f32[768]{0:T(1024)}, f32[768]{0:T(1024)}) all-reduce(f32[2,192]{1,0:T(2,128)S(1)} %pad_maximum_fusion, ...), channel_id=1, replica_groups=mesh['dp'=8,'tensor'=4] {'dp'}, use_global_device_ids=true, to_apply=%region_22.23 | all-reduce | flops 5760 | bytes 46080 | tf_op jit(solution)/shard_map/psum | solution.py:143
  1104.1 82.9 %all-reduce.16.cloned.1.call-done = (f32[768,3,192]{0,2,1:T(8,128)}, f32[192,768]{1,0:T(8,128)}, f32[768,768]{1,0:T(8,128)}, f32[768,768]{1,0:T(8,128)}) async-done(((f32[768,3,192]{0,2,1:T(8,128)}, f32[192,768]{1,0:T(8,128)}, f32[768,768]{1,0:T(8,128)}, f32[768,768]{1,0:T(8,128)}), (f32[768,3,192]{0,2,1:T(8,128)}, f32[192,768]{1,0:T(8,128)}, f32[768,768]{1,0:T(8,128)}, ...) | async-done | bytes 7077904 | tf_op jit(solution)/shard_map/psum | solution.py:143
  1187.0 2.9 copy.107
  1189.9 1.9 copy.108
  (191 shorter events, 52.3 us)
Async XLA Ops:
  7.2 272.2 %copy-start = (bf16[768,768]{1,0:T(8,128)(2,1)S(1)}, bf16[768,768]{1,0:T(8,128)(2,1)}, u32[]{:S(2)}) copy-start(bf16[768,768]{1,0:T(8,128)(2,1)} %param.27) | copy-start | bytes 3538948
  7.2 265.0 %all-reduce.8.cloned.1.call-start = ((), (), s32[]{:S(2)}) async-start(), calls=%async_computation | async-start | bytes 12582912 | tf_op jit(solution)/shard_map/psum | solution.py:91
  11.5 7.3 copy-start.32
  12.8 7.5 copy-start.27
  38.6 7.8 copy-start.10
  40.8 0.9 copy-start.6
  41.7 230.5 %copy-start.29 = (f32[768]{0:T(1024)S(1)}, f32[768]{0:T(1024)}, u32[]{:S(2)}) copy-start(f32[768]{0:T(1024)} %param.24) | copy-start | bytes 9220
  46.4 479.5 %all-reduce.10.cloned.1.call-start = ((), (), s32[]{:S(2)}) async-start(), calls=%async_computation.1 | async-start | bytes 12582912 | tf_op jit(solution)/shard_map/psum | solution.py:99
  276.8 2.7 copy-start.2
  276.8 0.9 copy-start.18
  276.8 0.9 copy-start.23
  277.7 1.8 copy-start.35
  279.4 18.3 %copy-start.12 = (bf16[2048,768]{1,0:T(8,128)(2,1)}, bf16[2048,768]{1,0:T(8,128)(2,1)S(1)}, u32[]{:S(2)}) copy-start(bf16[2048,768]{1,0:T(8,128)(2,1)S(1)} %fusion.69) | copy-start | bytes 9437188
  279.4 20.1 %copy-start.33 = (bf16[768,768]{1,0:T(8,128)(2,1)S(1)}, bf16[768,768]{1,0:T(8,128)(2,1)}, u32[]{:S(2)}) copy-start(bf16[768,768]{1,0:T(8,128)(2,1)} %param.29) | copy-start | bytes 3538948
  297.8 1.8 copy-start.37
  304.0 221.9 %copy-start.30 = (f32[768]{0:T(1024)S(1)}, f32[768]{0:T(1024)}, u32[]{:S(2)}) copy-start(f32[768]{0:T(1024)} %param.30) | copy-start | bytes 9220
  304.0 475.5 %all-reduce.12.cloned.1.call-start = ((), (), s32[]{:S(2)}) async-start(), calls=%async_computation.2 | async-start | bytes 12582912 | tf_op jit(solution)/shard_map/psum | solution.py:112
  531.6 1.9 copy-start.5
  531.6 1.9 copy-start.22
  532.5 4.6 copy-start.31
  533.5 8.5 slice-start.2
  537.1 4.9 copy-start.34
  537.1 4.9 slice-start.3
  542.0 9.4 copy-start.4
  542.0 237.5 %copy-start.19 = (f32[2048]{0:T(1024)}, f32[2048]{0:T(1024)S(1)}, u32[]{:S(2)}) copy-start(f32[2048]{0:T(1024)S(1)} %negate_multiply_fusion.2) | copy-start | bytes 24580
  551.4 1.7 copy-start.36
  557.6 512.5 %all-reduce.14.cloned.1.call-start = ((), (), s32[]{:S(2)}) async-start(), calls=%async_computation.3 | async-start | bytes 12582912 | tf_op jit(solution)/shard_map/psum | solution.py:142
  788.3 7.0 copy-start.16
  792.6 2.7 copy-start.3
  829.8 9.3 copy-start.8
  829.9 4.3 copy-start.11
  848.2 7.1 copy-start.20
  848.3 338.7 %all-reduce.16.cloned.1.call-start = ((), (), s32[]{:S(2)}) async-start(), calls=%async_computation.4 | async-start | bytes 14155776 | tf_op jit(solution)/shard_map/psum | solution.py:143
  848.3 7.1 copy-start.38
  848.3 14.2 %slice-start = ((s8[6291456]{0:T(1024)(128)(4,1)}), s8[4194304]{0:T(1024)(128)(4,1)S(1)}, s32[]{:S(2)}) async-start(s8[6291456]{0:T(1024)(128)(4,1)} %bitcast.157), calls=%async_computation.5 | async-start | bytes 8388608
  855.4 7.1 slice-start.1
  855.4 7.1 copy-start.7
  862.5 1.9 copy-start.13
  862.5 2.8 copy-start.17
  868.6 1.1 copy-start.9
  870.0 207.8 %copy-start.21 = (f32[768]{0:T(1024)S(1)}, f32[768]{0:T(1024)}, u32[]{:S(2)}) copy-start(f32[768]{0:T(1024)} %get-tuple-element.150) | copy-start | bytes 9220
  870.0 207.8 %copy-start.24 = (f32[768]{0:T(1024)S(1)}, f32[768]{0:T(1024)}, u32[]{:S(2)}) copy-start(f32[768]{0:T(1024)} %get-tuple-element.145) | copy-start | bytes 9220
  870.1 207.8 %copy-start.25 = (f32[768]{0:T(1024)S(1)}, f32[768]{0:T(1024)}, u32[]{:S(2)}) copy-start(f32[768]{0:T(1024)} %get-tuple-element.149) | copy-start | bytes 9220
  870.1 207.7 %copy-start.26 = (f32[768]{0:T(1024)S(1)}, f32[768]{0:T(1024)}, u32[]{:S(2)}) copy-start(f32[768]{0:T(1024)} %get-tuple-element.215) | copy-start | bytes 9220
  870.1 207.7 %copy-start.28 = (f32[768]{0:T(1024)S(1)}, f32[768]{0:T(1024)}, u32[]{:S(2)}) copy-start(f32[768]{0:T(1024)} %get-tuple-element.223) | copy-start | bytes 9220
  1187.0 4.9 copy-start.15
  1187.0 6.3 copy-start.14
  1187.0 7.7 copy-start.1
Sparse Core Ops, SparseCore 0:
  46.5 225.5 all-reduce.7
  304.1 221.7 all-reduce.9
  557.8 221.7 all-reduce.11
  848.4 221.7 all-reduce.13
  1074.8 112.0 all-reduce.15
where the time goes:
time: 1210 us; the launch traced here: 1200 us
  waiting for transfers between devices  952 us (79%)
  matrix products  106 us (9%)
  other arithmetic  55.1 us (5%)
  local copies, waits for them, and re-layouts  46.6 us (4%)
  blocking collectives  26.2 us (2%)
  between operations  14.8 us (1%)
    psum x1, waiting for transfers between devices, per_device(): attn = lax.psum(heads_part, 'tensor')  225 us
    psum x1, waiting for transfers between devices, per_device(): down = lax.psum(down_part, 'tensor')  222 us
    psum x1, waiting for transfers between devices, per_device(): d_hone = lax.psum(hone_part, 'tensor') + d_ztwo  222 us
    psum x1, waiting for transfers between devices, per_device(): d_inputs = lax.psum(input_part, 'tensor') + d_zone  200 us
    psum x1, waiting for transfers between devices, per_device(): lax.psum((d_wqkv, d_bqv, d_wout, d_bout, d_gone, d_sone, d_wup, d_bup, d_...  82.9 us
    psum x1, blocking collectives, per_device(): lax.psum((d_wqkv, d_bqv, d_wout, d_bout, d_gone, d_sone, d_wup, d_bup, d_...  26.2 us
  transfers between devices with their start and end apart: 5, of which 5 were waited for; matrix products, arithmetic and copies ran while one was open for 2% of the time, Pallas kernels for 0%

commit v1 on v0

--- a/solution.py
+++ b/solution.py
@@ -88,7 +88,9 @@
     context, log_total = lax.map(doc_forward, (queries_doc, keys_doc, values_doc, key_valid))
     context = context.reshape(rows, local_heads * HD)
     heads_part = jnp.dot(context, w_out, preferred_element_type=jnp.float32)
-    attn = lax.psum(heads_part, "tensor")
+    attn = heads_part
+    for hop in (1, 2):
+        attn = attn + lax.ppermute(attn, "tensor", [(dev, dev ^ hop) for dev in range(4)])
     z_one = inputs.astype(jnp.float32) + attn + b_out
     h_one, pull_one = jax.vjp(norm_layer, z_one, g_one, s_one)
     h_low = h_one.astype(jnp.bfloat16)

time: 1210 us -> 1400 us (1.16)
  waiting for transfers between devices: 952 us -> 1110 us
  local copies, waits for them, and re-layouts: 46.6 us -> 66.8 us
    ppermute x0 -> x2, waiting for transfers between devices: none -> 401 us  [per_device(): lax.ppermute(attn, 'tensor', [(dev, dev ^ hop) for dev in range(4)])]
    psum x1 -> x0, waiting for transfers between devices: 225 us -> none  [per_device(): attn = lax.psum(heads_part, 'tensor')]
    unnamed x94 -> x88, local copies, waits for them, and re-layouts: 21.4 us -> 41.7 us
  transfers between devices with their start and end apart: 5 -> 6, of which waited for: 5 -> 6; matrix products, arithmetic and copies ran while one was open for 2% -> 4% of each run, Pallas kernels for 0% -> 0%
where the time goes in v1:
time: 1400 us; the launch traced here: 1390 us
  waiting for transfers between devices  1110 us (79%)
  matrix products  104 us (7%)
  local copies, waits for them, and re-layouts  66.8 us (5%)
  other arithmetic  61.7 us (4%)
  blocking collectives  25.9 us (2%)
  between operations  14.7 us (1%)
    ppermute x2, waiting for transfers between devices, per_device(): lax.ppermute(attn, 'tensor', [(dev, dev ^ hop) for dev in range(4)])  401 us
    psum x1, waiting for transfers between devices, per_device(): d_hone = lax.psum(hone_part, 'tensor') + d_ztwo  222 us
    psum x1, waiting for transfers between devices, per_device(): down = lax.psum(down_part, 'tensor')  219 us
    psum x1, waiting for transfers between devices, per_device(): d_inputs = lax.psum(input_part, 'tensor') + d_zone  196 us
    psum x1, waiting for transfers between devices, per_device(): lax.psum((d_wqkv, d_bqv, d_wout, d_bout, d_gone, d_sone, d_wup, d_bup, d_...  76.1 us
    unnamed x88, local copies, waits for them, and re-layouts  41.7 us
  transfers between devices with their start and end apart: 6, of which 6 were waited for; matrix products, arithmetic and copies ran while one was open for 4% of the time, Pallas kernels for 0%

profile of v1, /device:TPU:0, one launch (start us, length us, event | category | flops | bytes accessed | tf_op | source)
XLA Modules:
  0.0 1393.2 jit_solution(12779254341649545562)
XLA Ops:
  7.2 4.2 fusion.90
  13.5 3.1 squeeze.34
  16.6 2.2 squeeze.35
  21.1 2.9 fusion.73
  25.0 13.6 while.26
  38.6 2.0 copy.57
  40.8 2.2 fusion.91
  43.0 3.1 collective-permute-start
  46.1 135.5 %collective-permute-done = f32[2048,768]{0,1:T(8,128)S(1)} collective-permute-done((f32[2048,768]{0,1:T(8,128)S(1)}, f32[2048,768]{0,1:T(8,128)S(1)}, u32[]{:S(2)}, u32[]{:S(2)}) %collective-permute-start) | collective-permute-done | bytes 6291488 | tf_op jit(solution)/shard_map/ppermute | solution.py:93
  181.6 4.0 add.159
  185.6 2.8 collective-permute-start.1
  188.4 4.8 copy.53
  193.2 265.1 %collective-permute-done.1 = f32[2048,768]{0,1:T(8,128)} collective-permute-done((f32[2048,768]{0,1:T(8,128)}, f32[2048,768]{0,1:T(8,128)}, u32[]{:S(2)}, u32[]{:S(2)}) %collective-permute-start.1) | collective-permute-done | bytes 6291488 | tf_op jit(solution)/shard_map/ppermute | solution.py:93
  458.4 7.5 fusion.88
  468.5 18.6 %multiply_convert_fusion.2 = (bf16[2048,768]{1,0:T(8,128)(2,1)S(1)}, f32[2048,768]{1,0:T(8,128)}, f32[2048,768]{1,0:T(8,128)}) fusion(f32[768]{0:T(1024)S(1)} %copy-done.30, bf16[2048,768]{0,1:T(8,128)(2,1)S(1)} %fusion.69, bf16[768,768]{1,0:T(8,128)(2,1)S(1)} %copy-done), kind=kOutput, calls=%fused_computation.84 | convolution fusion | flops 2519728128 | bytes 20057088 | tf_op jit(solution)/shard_map/dot_general | solution.py:97
  488.9 4.5 fusion.92
  493.5 5.0 copy.59
  498.5 218.9 %all-reduce.7.cloned.1.call-done = f32[2048,768]{0,1:T(8,128)} async-done(((f32[2048,768]{0,1:T(8,128)}), f32[2048,768]{0,1:T(8,128)}) %all-reduce.7.cloned.1.call-update) | async-done | bytes 6291472 | tf_op jit(solution)/shard_map/psum | solution.py:101
  717.5 5.6 fusion.86
  724.9 3.7 multiply_reduce_fusion.1
  728.7 5.1 fusion.85
  733.9 10.0 convert_reduce_fusion
  745.6 4.5 fusion.93
  750.1 221.8 %all-reduce.9.cloned.1.call-done = f32[2048,768]{0,1:T(8,128)} async-done(((f32[2048,768]{0,1:T(8,128)}), f32[2048,768]{0,1:T(8,128)}) %all-reduce.9.cloned.1.call-update) | async-done | bytes 6291472 | tf_op jit(solution)/shard_map/psum | solution.py:114
  972.0 8.7 multiply_reduce_fusion.2
  980.7 3.9 fusion.84
  984.6 2.7 copy-done.3
  990.9 30.5 %while.27 = (s32[]{:T(128)}, bf16[4,512,3,64]{1,3,2,0:T(8,128)(2,1)S(1)}, bf16[4,512,3,64]{1,3,2,0:T(8,128)(2,1)}, bf16[4,512,3,64]{1,3,2,0:T(8,128)(2,1)S(1)}, ...) while((s32[]{:T(128)}, ...), condition=%wide.region_16.17_spmd, body=%wide.region_14.16_spmd.sunk | while | flops 513047040 | bytes 25611892 | solution.py:130
  992.3 2.0 multiply_reduce_fusion.8
  999.9 2.0 multiply_reduce_fusion.8
  1007.5 2.0 multiply_reduce_fusion.8
  1012.0 1.7 fusion.147
  1015.1 2.0 multiply_reduce_fusion.8
  1023.6 2.1 constant_dynamic-update-slice_fusion.2
  1028.3 2.3 stack_reshape.7
  1032.5 7.2 convolution_bitcast_fusion
  1039.8 7.0 fusion.94
  1046.8 7.0 fusion.78
  1053.9 2.0 fusion.80
  1056.7 3.2 fusion.75
  1059.9 4.9 copy.67
  1065.4 196.2 %all-reduce.11.cloned.1.call-done = f32[2048,768]{0,1:T(8,128)} async-done(((f32[2048,768]{0,1:T(8,128)}), f32[2048,768]{0,1:T(8,128)}) %all-reduce.11.cloned.1.call-update) | async-done | bytes 6291472 | tf_op jit(solution)/shard_map/psum | solution.py:144
  1261.7 8.0 add_reduce_fusion
  1269.6 7.0 copy.68
  1276.6 25.9 %all-reduce = (f32[2,192]{1,0:T(2,128)}, f32[768]{0:T(1024)}, f32[768]{0:T(1024)}, f32[768]{0:T(1024)}, f32[768]{0:T(1024)}, /*index=5*/f32[768]{0:T(1024)}, f32[768]{0:T(1024)}, f32[768]{0:T(1024)}) all-reduce(f32[2,192]{1,0:T(2,128)S(1)} %pad_maximum_fusion, ...), channel_id=1, replica_groups=mesh['dp'=8,'tensor'=4] {'dp'}, use_global_device_ids=true, to_apply=%region_21.22 | all-reduce | flops 5760 | bytes 46080 | tf_op jit(solution)/shard_map/psum | solution.py:145
  1302.5 76.1 %all-reduce.13.cloned.1.call-done = (f32[768,3,192]{0,2,1:T(8,128)}, f32[192,768]{1,0:T(8,128)}, f32[768,768]{1,0:T(8,128)}, f32[768,768]{1,0:T(8,128)}) async-done(((f32[768,3,192]{0,2,1:T(8,128)}, f32[192,768]{1,0:T(8,128)}, f32[768,768]{1,0:T(8,128)}, f32[768,768]{1,0:T(8,128)}), (f32[768,3,192]{0,2,1:T(8,128)}, f32[192,768]{1,0:T(8,128)}, f32[768,768]{1,0:T(8,128)}, ...) | async-done | bytes 7077904 | tf_op jit(solution)/shard_map/psum | solution.py:145
  1378.6 2.9 copy.124
  1381.5 1.9 copy.125
  (187 shorter events, 62.0 us)
Async XLA Ops:
  7.2 461.3 %copy-start = (bf16[768,768]{1,0:T(8,128)(2,1)S(1)}, bf16[768,768]{1,0:T(8,128)(2,1)}, u32[]{:S(2)}) copy-start(bf16[768,768]{1,0:T(8,128)(2,1)} %param.27) | copy-start | bytes 3538948
  7.2 710.3 %all-reduce.7.cloned.1.call-start = ((), (), s32[]{:S(2)}) async-start(), calls=%async_computation | async-start | bytes 12582912 | tf_op jit(solution)/shard_map/psum | solution.py:101
  11.5 7.3 copy-start.27
  12.8 7.5 copy-start.22
  38.6 4.4 copy-start.10
  40.8 144.9 %copy-start.6 = (bf16[24,8,4,512]{3,1,2,0:T(8,128)(2,1)}, bf16[24,8,4,512]{3,1,2,0:T(8,128)(2,1)S(1)}, u32[]{:S(2)}) copy-start(bf16[24,8,4,512]{3,1,2,0:T(8,128)(2,1)S(1)} %copy.77) | copy-start | bytes 2359300
  43.0 138.6 %collective-permute-start = (f32[2048,768]{0,1:T(8,128)S(1)}, f32[2048,768]{0,1:T(8,128)S(1)}, u32[]{:S(2)}, u32[]{:S(2)}) collective-permute-start(f32[2048,768]{0,1:T(8,128)S(1)} %fusion.91), channel_id=1, source_target_pairs={{0,1},{1,0},{2,3},{3,2},{4,5},{5,4},{6,7},{7,6},{8,9},{9,8},{10,11... | collective-permute-start | bytes 18874376 | tf_op jit(solution)/shard_map/ppermute | solution.py:93
  185.6 272.7 %copy-start.24 = (f32[768]{0:T(1024)S(1)}, f32[768]{0:T(1024)}, u32[]{:S(2)}) copy-start(f32[768]{0:T(1024)} %param.24) | copy-start | bytes 9220
  185.6 272.7 %collective-permute-start.1 = (f32[2048,768]{0,1:T(8,128)}, f32[2048,768]{0,1:T(8,128)}, u32[]{:S(2)}, u32[]{:S(2)}) collective-permute-start(f32[2048,768]{0,1:T(8,128)} %add.159), channel_id=1, source_target_pairs={{0,2},{1,3},{2,0},{3,1},{4,6},{5,7},{6,4},{7,5},{8,10},{9,11},{10,... | collective-permute-start | bytes 18874376 | tf_op jit(solution)/shard_map/ppermute | solution.py:93
  465.8 2.7 copy-start.2
  465.8 0.8 copy-start.18
  465.8 0.8 copy-start.21
  466.6 1.9 copy-start.30
  468.5 18.6 %copy-start.13 = (bf16[2048,768]{0,1:T(8,128)(2,1)}, bf16[2048,768]{0,1:T(8,128)(2,1)S(1)}, u32[]{:S(2)}) copy-start(bf16[2048,768]{0,1:T(8,128)(2,1)S(1)} %fusion.69) | copy-start | bytes 9437188
  468.5 20.4 %copy-start.28 = (bf16[768,768]{1,0:T(8,128)(2,1)S(1)}, bf16[768,768]{1,0:T(8,128)(2,1)}, u32[]{:S(2)}) copy-start(bf16[768,768]{1,0:T(8,128)(2,1)} %param.29) | copy-start | bytes 3538948
  487.1 1.8 copy-start.32
  493.4 224.1 %copy-start.25 = (f32[768]{0:T(1024)S(1)}, f32[768]{0:T(1024)}, u32[]{:S(2)}) copy-start(f32[768]{0:T(1024)} %param.30) | copy-start | bytes 9220
  493.4 478.6 %all-reduce.9.cloned.1.call-start = ((), (), s32[]{:S(2)}) async-start(), calls=%async_computation.1 | async-start | bytes 12582912 | tf_op jit(solution)/shard_map/psum | solution.py:114
  723.0 1.9 copy-start.4
  723.1 1.9 copy-start.20
  723.8 4.9 copy-start.26
  724.9 8.9 slice-start.2
  728.7 5.2 copy-start.29
  728.7 5.2 slice-start.3
  733.9 10.0 copy-start.5
  743.9 1.7 copy-start.31
  750.1 511.6 %all-reduce.11.cloned.1.call-start = ((), (), s32[]{:S(2)}) async-start(), calls=%async_computation.2 | async-start | bytes 12582912 | tf_op jit(solution)/shard_map/psum | solution.py:144
  980.7 6.6 copy-start.16
  984.6 2.7 copy-start.3
  1021.4 9.3 copy-start.8
  1021.4 4.3 copy-start.12
  1039.7 338.8 %all-reduce.13.cloned.1.call-start = ((), (), s32[]{:S(2)}) async-start(), calls=%async_computation.3 | async-start | bytes 14155776 | tf_op jit(solution)/shard_map/psum | solution.py:145
  1039.8 7.0 copy-start.33
  1039.8 14.0 %slice-start = ((s8[6291456]{0:T(1024)(128)(4,1)}), s8[4194304]{0:T(1024)(128)(4,1)S(1)}, s32[]{:S(2)}) async-start(s8[6291456]{0:T(1024)(128)(4,1)} %bitcast.157), calls=%async_computation.4 | async-start | bytes 8388608
  1046.8 7.0 slice-start.1
  1046.8 7.0 copy-start.7
  1053.8 2.0 copy-start.11
  1053.9 2.8 copy-start.17
  1059.9 5.2 copy-start.9
  1269.6 7.0 copy-start.19
  1269.6 7.0 copy-start.23
  1378.5 4.9 copy-start.15
  1378.6 6.3 copy-start.14
  1378.6 7.7 copy-start.1
Sparse Core Ops, SparseCore 0:
  493.5 223.8 all-reduce.6
  750.2 221.7 all-reduce.8
  1039.9 221.7 all-reduce.10
  1266.3 112.1 all-reduce.12
